TPU v7x, 512 devices: a whole 4x8x8 slice. The times are simulated.
512 devices in a mesh: au: 32 (over z, y_lo), ia: 16 (over x, y_hi, core).
Axes of the slice: x: 4, y: 8 (y_hi: 2, y_lo: 4; y = y_hi * 4 + y_lo), z: 8, core: 2. Of those that a mesh axis runs over, the one named last changes fastest.
Arguments:
- user_emb: bfloat16 [32, 2048, 256], P('au', 'ia'), may hold values from -6 to 6
- item_emb: bfloat16 [16, 1024, 256], P('ia', 'au'), may hold values from -6 to 6
- weight: bfloat16 [256, 256], replicated, may hold values from -0.375 to 0.375
- grad_user: bfloat16 [32, 2048, 256], P('au', 'ia'), may hold values from -6 to 6
- grad_item: bfloat16 [16, 1024, 256], P('ia', 'au'), may hold values from -6 to 6
- tile_values: bfloat16 [32, 2048, 128, 128], P('au', 'ia'), may hold values from 0 to 1
- tile_rows: int32 [32, 2048], P('au', 'ia'), may hold values from 0 to 15
- tile_cols: int32 [32, 2048], P('au', 'ia'), may hold values from 0 to 7
- tile_norm: int32 [32, 2048], P('au', 'ia'), may hold values from 32 to 128
- tile_count: int32 [32, 16], P('au', 'ia'), may hold values from 64 to 128, as said below
Outputs:
- grad_user_emb: bfloat16 [32, 2048, 256], P('au', 'ia')
- grad_item_emb: bfloat16 [16, 1024, 256], P('ia', 'au')
- grad_weight: float32 [256, 256], replicated
Inputs may be any that keep to these rules, and one draw needn't show every extreme that they name: `tile_rows`: slots of one block pair may name the same tile position; their terms add. Slots at and after tile_count[a, b] are unused; some block pair has exactly 128 live slots in every draw.
All inputs are finite; a program needn't handle non-finite values.
Results may differ from a plain program's by a relative error of at most 0.025.
Values may be sent and summed in bfloat16 or wider, within the bound.
No kernel may reach another device: no remote copies, remote signals or barrier semaphores. Data moves between devices by JAX's collectives and lax.ppermute only.
A program may use at most 64 MiB of HBM per device.

v0:
```python
import math
import jax
import jax.numpy as jnp
from jax import lax
from jax.sharding import PartitionSpec as P

slot_group = 8


def from_everyone(value, axis):
    copies = jnp.broadcast_to(value, (lax.axis_size(axis), *value.shape))
    return lax.all_to_all(copies, axis, split_axis=0, concat_axis=0, tiled=True)


def in_order(pieces, dim):
    pieces = jnp.moveaxis(pieces, 0, dim)
    shape = pieces.shape
    return pieces.reshape(*shape[:dim], shape[dim] * shape[dim + 1], *shape[dim + 2 :])


def collect(value, axis, dim):
    pieces = from_everyone(value, axis)
    return in_order(pieces, dim)


def in_blocks(value, dim, peers):
    shape = value.shape
    pieces = value.reshape(*shape[:dim], peers, shape[dim] // peers, *shape[dim + 1 :])
    return jnp.moveaxis(pieces, dim, 0)


def summed_on_arrival(value, axis, dim):
    pieces = in_blocks(value, dim, lax.axis_size(axis))
    arrived = lax.all_to_all(pieces, axis, split_axis=0, concat_axis=0, tiled=True)
    return arrived.astype(jnp.float32).sum(axis=0)


def split_tiles(block, edge):
    return block.reshape(-1, edge, block.shape[-1])


def fetch_items(grad_item, edge):
    cotangent = collect(grad_item, "au", 1)
    return (split_tiles(cotangent[0], edge), None)


def fetch_users(grad_user, edge):
    cotangent = collect(grad_user, "ia", 1)
    return (split_tiles(cotangent[0], edge), None)


def sweep(
    tile_block,
    row_ids,
    col_ids,
    norm_ids,
    live_count,
    item_source,
    user_source,
    user_shape,
    item_shape,
):
    turn_count = (live_count + slot_group - 1) // slot_group
    placeholder = jnp.zeros((1,), jnp.float32)

    def one_turn(turn_index, totals):
        user_total, item_total = totals
        first_slot = turn_index * slot_group
        values = lax.dynamic_slice_in_dim(tile_block, first_slot, slot_group, 0)
        row_pick = lax.dynamic_slice_in_dim(row_ids, first_slot, slot_group, 0)
        col_pick = lax.dynamic_slice_in_dim(col_ids, first_slot, slot_group, 0)
        norm_pick = lax.dynamic_slice_in_dim(norm_ids, first_slot, slot_group, 0)
        live_mask = first_slot + jnp.arange(slot_group, dtype=jnp.int32) < live_count
        inverse = jnp.where(live_mask, 1.0 / norm_pick.astype(jnp.float32), 0.0)[:, None, None]
        if item_source is not None:
            forward = jnp.einsum(
                "gic,gcd->gid", values, item_source[col_pick], preferred_element_type=jnp.float32
            )
            user_total = user_total.at[row_pick].add(forward * inverse)
        if user_source is not None:
            backward = jnp.einsum(
                "gic,gid->gcd", values, user_source[row_pick], preferred_element_type=jnp.float32
            )
            item_total = item_total.at[col_pick].add(backward * inverse)
        return (user_total, item_total)

    start = (
        jnp.zeros(user_shape, jnp.float32) if item_source is not None else placeholder,
        jnp.zeros(item_shape, jnp.float32) if user_source is not None else placeholder,
    )
    return lax.fori_loop(0, turn_count, one_turn, start)


def reduce_users(user_total, width):
    return summed_on_arrival(user_total.reshape(-1, width).astype(jnp.bfloat16), "ia", 0)


def reduce_items(item_total, width):
    return summed_on_arrival(item_total.reshape(-1, width).astype(jnp.bfloat16), "au", 0)


def block_product(embedded, total):
    return jnp.einsum(
        "rd,re->de", embedded.astype(jnp.float32), total, precision=lax.Precision.HIGHEST
    )


def per_device(
    user_emb,
    item_emb,
    weight,
    grad_user,
    grad_item,
    tile_values,
    tile_rows,
    tile_cols,
    tile_norm,
    tile_count,
):
    width = weight.shape[0]
    edge = tile_values.shape[2]
    user_shape = (user_emb.shape[1] * lax.axis_size("ia") // edge, edge, width)
    item_shape = (item_emb.shape[1] * lax.axis_size("au") // edge, edge, width)
    tile_block = tile_values[0]
    row_ids = tile_rows[0]
    col_ids = tile_cols[0]
    norm_ids = tile_norm[0]
    live_count = tile_count[0, 0]
    item_source, item_rows = fetch_items(grad_item, edge)
    user_total, unused = sweep(
        tile_block,
        row_ids,
        col_ids,
        norm_ids,
        live_count,
        item_source,
        None,
        user_shape,
        item_shape,
    )
    q_user = reduce_users(user_total, width)
    user_source, user_rows = fetch_users(grad_user, edge)
    unused, item_total = sweep(
        tile_block,
        row_ids,
        col_ids,
        norm_ids,
        live_count,
        None,
        user_source,
        user_shape,
        item_shape,
    )
    q_item = reduce_items(item_total, width)
    weight_part = block_product(user_emb[0], q_user) + block_product(item_emb[0], q_item)
    user_count = user_emb.shape[1] * lax.axis_size("ia") * lax.axis_size("au")
    item_count = item_emb.shape[1] * lax.axis_size("au") * lax.axis_size("ia")
    grad_weight = lax.psum(weight_part, ("au", "ia")) / math.sqrt(user_count + item_count)
    grad_user_emb = jnp.einsum(
        "re,de->rd", q_user.astype(jnp.bfloat16), weight, preferred_element_type=jnp.float32
    ).astype(jnp.bfloat16)
    grad_item_emb = jnp.einsum(
        "re,de->rd", q_item.astype(jnp.bfloat16), weight, preferred_element_type=jnp.float32
    ).astype(jnp.bfloat16)
    return (grad_user_emb[None], grad_item_emb[None], grad_weight)


def solution(mesh):
    return jax.shard_map(
        per_device,
        mesh=mesh,
        in_specs=(
            P("au", "ia", None),
            P("ia", "au", None),
            P(),
            P("au", "ia", None),
            P("ia", "au", None),
            P("au", "ia", None, None),
            P("au", "ia"),
            P("au", "ia"),
            P("au", "ia"),
            P("au", "ia"),
        ),
        out_specs=(P("au", "ia", None), P("ia", "au", None), P()),
        check_vma=False,
    )
```

profile of v0, /device:TPU:23, one launch (start us, length us, event | category | flops | bytes accessed | tf_op | source)
XLA Modules:
  0.0 567.4 jit_solution(4700820097756876434)
XLA Ops:
  7.2 2.0 broadcast_in_dim.43
  9.2 8.5 %all-to-all-start.2 = ((bf16[16,1,128,256]{3,2,1,0:T(8,128)(2,1)}), bf16[16,1,128,256]{3,2,1,0:T(8,128)(2,1)}, u32[]{:S(2)}, u32[]{:S(2)}) async-start(bf16[16,1,128,256]{3,2,1,0:T(8,128)(2,1)} %broadcast_in_dim.43), calls=%async_computation.2 | async-start | bytes 2097152 | tf_op jit(solution)/shard_map/all_to_all | solution.py:12
  18.4 6.4 %copy.16 = bf16[1,128,128,128]{2,3,1,0:T(8,128)(2,1)} copy(bf16[1,128,128,128]{3,2,1,0:T(8,128)(2,1)} %param.19) | data formatting | bytes 8388608 | tf_op args[5]
  24.8 21.8 %all-to-all-done.2 = bf16[16,1,128,256]{3,2,1,0:T(8,128)(2,1)} async-done(((bf16[16,1,128,256]{3,2,1,0:T(8,128)(2,1)}), bf16[16,1,128,256]{3,2,1,0:T(8,128)(2,1)}, u32[]{:S(2)}, u32[]{:S(2)}) %all-to-all-start.2) | async-done | bytes 1048608 | tf_op jit(solution)/shard_map/all_to_all | solution.py:12
  47.4 12.4 %all-to-all-start = ((bf16[32,1,32,256]{3,2,1,0:T(8,128)(2,1)}), bf16[32,1,32,256]{3,2,1,0:T(8,128)(2,1)S(1)}, u32[]{:S(2)}, u32[]{:S(2)}) async-start(bf16[32,1,32,256]{3,2,1,0:T(8,128)(2,1)} %broadcast_in_dim.40), calls=%async_computation | async-start | bytes 1048576 | tf_op jit(solution)/shard_map/all_to_all | solution.py:12
  59.9 68.0 %while.21 = (s32[]{:T(128)}, f32[8,128,256]{2,1,0:T(8,128)S(1)}, s32[]{:T(128)}, s32[128]{0:T(128)S(1)}, bf16[128,128,128]{1,2,0:T(8,128)(2,1)}, /*index=5*/s32[...) while((s32[]{:T(128)}, f32[8,128,256]{2,1,0:T(8,128)S(1)}, ...), condition=%wide.region_6.7_spmd, body=%wide.region_4.6_spmd.sunk | while | flops 67634272 | bytes 6033919 | solution.py:91
  60.8 1.8 gather_fusion.1
  66.0 1.8 gather_fusion.1
  71.2 1.8 gather_fusion.1
  76.5 1.8 gather_fusion.1
  81.7 1.8 gather_fusion.1
  86.9 1.8 gather_fusion.1
  92.2 1.8 gather_fusion.1
  128.8 24.3 %all-to-all-start.3 = ((bf16[32,32,256]{2,1,0:T(8,128)(2,1)}), bf16[32,32,256]{2,1,0:T(8,128)(2,1)S(1)}, u32[]{:S(2)}, u32[]{:S(2)}) async-start(bf16[32,32,256]{2,1,0:T(8,128)(2,1)} %bitcast.11), calls=%async_computation.3 | async-start | bytes 1048576 | tf_op jit(solution)/shard_map/all_to_all | solution.py:34
  154.7 77.1 %while.20 = (s32[]{:T(128)}, f32[16,128,256]{2,1,0:T(8,128)}, s32[]{:T(128)}, s32[128]{0:T(128)S(1)}, bf16[128,128,128]{2,1,0:T(8,128)(2,1)}, /*index=5*/s32[128...) while((s32[]{:T(128)}, f32[16,128,256]{2,1,0:T(8,128)}, ...), condition=%wide.region_2.3_spmd, body=%wide.region_0.2_spmd.sunk | while | flops 67634272 | bytes 6033919 | solution.py:91
  157.3 3.3 scatter_fusion
  163.2 3.3 scatter_fusion
  169.2 3.3 scatter_fusion
  175.1 3.3 scatter_fusion
  181.0 3.3 scatter_fusion
  187.0 3.3 scatter_fusion
  192.9 3.2 scatter_fusion
  198.8 3.3 scatter_fusion
  204.7 3.3 scatter_fusion
  210.6 3.3 scatter_fusion
  216.6 3.3 scatter_fusion
  222.6 3.3 scatter_fusion
  228.5 3.3 scatter_fusion
  231.8 2.7 convert_element_type.37
  234.5 23.4 %all-to-all-start.1 = ((bf16[16,128,256]{2,1,0:T(8,128)(2,1)}), bf16[16,128,256]{2,1,0:T(8,128)(2,1)S(1)}, u32[]{:S(2)}, u32[]{:S(2)}) async-start(bf16[16,128,256]{2,1,0:T(8,128)(2,1)} %convert_element_type.37), calls=%async_computation.1 | async-start | bytes 2097152 | tf_op jit(solution)/shard_map/all_to_all | solution.py:34
  258.3 27.8 %all-to-all-done.1 = bf16[16,128,256]{2,1,0:T(8,128)(2,1)S(1)} async-done(((bf16[16,128,256]{2,1,0:T(8,128)(2,1)}), bf16[16,128,256]{2,1,0:T(8,128)(2,1)S(1)}, u32[]{:S(2)}, u32[]{:S(2)}) %all-to-all-start.1) | async-done | bytes 1048608 | tf_op jit(solution)/shard_map/all_to_all | solution.py:34
  289.0 269.7 %all-reduce.2.cloned.1.call-done = f32[256,256]{0,1:T(8,128)} async-done(((f32[256,256]{0,1:T(8,128)}), f32[256,256]{0,1:T(8,128)}) %all-reduce.2.cloned.1.call-update) | async-done | bytes 262160 | tf_op jit(solution)/shard_map/psum | solution.py:158
  (166 shorter events, 97.3 us)
Async XLA Ops:
  7.2 280.2 %copy-start = (bf16[256,256]{1,0:T(8,128)(2,1)S(1)}, bf16[256,256]{1,0:T(8,128)(2,1)}, u32[]{:S(2)}) copy-start(bf16[256,256]{1,0:T(8,128)(2,1)} %param.16) | copy-start | bytes 393220
  9.2 37.4 %all-to-all-start.2 = ((bf16[16,1,128,256]{3,2,1,0:T(8,128)(2,1)}), bf16[16,1,128,256]{3,2,1,0:T(8,128)(2,1)}, u32[]{:S(2)}, u32[]{:S(2)}) async-start(bf16[16,1,128,256]{3,2,1,0:T(8,128)(2,1)} %broadcast_in_dim.43), calls=%async_computation.2 | async-start | bytes 2097152 | tf_op jit(solution)/shard_map/all_to_all | solution.py:12
  18.4 28.2 %copy-start.5 = (bf16[1,32,256]{2,1,0:T(8,128)(2,1)S(1)}, bf16[1,32,256]{2,1,0:T(8,128)(2,1)}, u32[]{:S(2)}) copy-start(bf16[1,32,256]{2,1,0:T(8,128)(2,1)} %param.18) | copy-start | bytes 49156
  24.7 35.2 %copy-start.2 = (s32[1,128]{1,0:T(1,128)S(1)}, s32[1,128]{1,0:T(1,128)}, u32[]{:S(2)}) copy-start(s32[1,128]{1,0:T(1,128)} %param.20) | copy-start | bytes 1540
  24.8 35.2 %copy-start.3 = (s32[1,128]{1,0:T(1,128)S(1)}, s32[1,128]{1,0:T(1,128)}, u32[]{:S(2)}) copy-start(s32[1,128]{1,0:T(1,128)} %param.21) | copy-start | bytes 1540
  24.8 35.2 %copy-start.4 = (s32[1,128]{1,0:T(1,128)S(1)}, s32[1,128]{1,0:T(1,128)}, u32[]{:S(2)}) copy-start(s32[1,128]{1,0:T(1,128)} %param.22) | copy-start | bytes 1540
  47.4 81.4 %all-to-all-start = ((bf16[32,1,32,256]{3,2,1,0:T(8,128)(2,1)}), bf16[32,1,32,256]{3,2,1,0:T(8,128)(2,1)S(1)}, u32[]{:S(2)}, u32[]{:S(2)}) async-start(bf16[32,1,32,256]{3,2,1,0:T(8,128)(2,1)} %broadcast_in_dim.40), calls=%async_computation | async-start | bytes 1048576 | tf_op jit(solution)/shard_map/all_to_all | solution.py:12
  128.8 105.7 %all-to-all-start.3 = ((bf16[32,32,256]{2,1,0:T(8,128)(2,1)}), bf16[32,32,256]{2,1,0:T(8,128)(2,1)S(1)}, u32[]{:S(2)}, u32[]{:S(2)}) async-start(bf16[32,32,256]{2,1,0:T(8,128)(2,1)} %bitcast.11), calls=%async_computation.3 | async-start | bytes 1048576 | tf_op jit(solution)/shard_map/all_to_all | solution.py:34
  234.5 23.5 %copy-start.6 = (bf16[1,32,256]{2,1,0:T(8,128)(2,1)S(1)}, bf16[1,32,256]{2,1,0:T(8,128)(2,1)}, u32[]{:S(2)}) copy-start(bf16[1,32,256]{2,1,0:T(8,128)(2,1)} %param.15) | copy-start | bytes 49156
  234.5 51.8 %copy-start.1 = (bf16[1,128,256]{2,1,0:T(8,128)(2,1)S(1)}, bf16[1,128,256]{2,1,0:T(8,128)(2,1)}, u32[]{:S(2)}) copy-start(bf16[1,128,256]{2,1,0:T(8,128)(2,1)} %param.14) | copy-start | bytes 196612
  234.5 51.7 %all-to-all-start.1 = ((bf16[16,128,256]{2,1,0:T(8,128)(2,1)}), bf16[16,128,256]{2,1,0:T(8,128)(2,1)S(1)}, u32[]{:S(2)}, u32[]{:S(2)}) async-start(bf16[16,128,256]{2,1,0:T(8,128)(2,1)} %convert_element_type.37), calls=%async_computation.1 | async-start | bytes 2097152 | tf_op jit(solution)/shard_map/all_to_all | solution.py:34
  257.9 300.8 %all-reduce.2.cloned.1.call-start = ((), (), s32[]{:S(2)}) async-start(), calls=%async_computation.4 | async-start | bytes 524288 | tf_op jit(solution)/shard_map/psum | solution.py:158
Sparse Core Ops, SparseCore 0:
  287.5 271.1 all-reduce.1
where the time goes:
time: 570 us; the launch traced here: 567 us
  waiting for transfers between devices  319 us (56%)
  other arithmetic  85.7 us (15%)
  starting transfers between devices  68.7 us (12%)
  local copies, waits for them, and re-layouts  42.9 us (8%)
  matrix products  35.1 us (6%)
  between operations  14.8 us (3%)
    psum x1, waiting for transfers between devices, per_device(): lax.psum(weight_part, ('au', 'ia')) / math.sqrt(user_count + item_count)  270 us
    all_to_all x2, starting transfers between devices, summed_on_arrival(): lax.all_to_all(pieces, axis, split_axis=0, concat_axis=0, tiled=True)  47.7 us
    scatter-add x13, other arithmetic, one_turn(): user_total = user_total.at[row_pick].add(forward * inverse)  42.8 us
    all_to_all x2, waiting for transfers between devices, summed_on_arrival(): lax.all_to_all(pieces, axis, split_axis=0, concat_axis=0, tiled=True)  27.8 us
    gather x13, local copies, waits for them, and re-layouts, one_turn(): user_source[row_pick]  23.5 us
    all_to_all x2, waiting for transfers between devices, from_everyone(): return lax.all_to_all(copies, axis, split_axis=0, concat_axis=0, tiled=True)  21.8 us
    all_to_all x2, starting transfers between devices, from_everyone(): return lax.all_to_all(copies, axis, split_axis=0, concat_axis=0, tiled=True)  20.9 us
    select_n x26, other arithmetic, one_turn(): jnp.where(live_mask, 1.0 / norm_pick.astype(jnp.float32), 0.0)  18.8 us
  transfers between devices with their start and end apart: 5, of which 3 were waited for; matrix products, arithmetic and copies ran while one was open for 28% of the time, Pallas kernels for 0%

commit v1 on v0

--- a/solution.py
+++ b/solution.py
@@ -5,6 +5,11 @@
 from jax.sharding import PartitionSpec as P
 
 slot_group = 8
+
+
+def process_desk(x_in, shard_axis, link_axis):
+    carry_in = lax.psum(lax.psum(x_in, shard_axis), link_axis)
+    return carry_in
 
 
 def from_everyone(value, axis):
@@ -155,7 +160,7 @@
     weight_part = block_product(user_emb[0], q_user) + block_product(item_emb[0], q_item)
     user_count = user_emb.shape[1] * lax.axis_size("ia") * lax.axis_size("au")
     item_count = item_emb.shape[1] * lax.axis_size("au") * lax.axis_size("ia")
-    grad_weight = lax.psum(weight_part, ("au", "ia")) / math.sqrt(user_count + item_count)
+    grad_weight = process_desk(weight_part, "ia", "au") / math.sqrt(user_count + item_count)
     grad_user_emb = jnp.einsum(
         "re,de->rd", q_user.astype(jnp.bfloat16), weight, preferred_element_type=jnp.float32
     ).astype(jnp.bfloat16)

time: 570 us -> 796 us (1.40)
  the two profiles are of different devices: /device:TPU:23 before, /device:TPU:2 now
where the time goes in v1:
time: 796 us; the launch traced here: 793 us
  waiting for transfers between devices  545 us (68%)
  other arithmetic  97.9 us (12%)
  local copies, waits for them, and re-layouts  47.7 us (6%)
  starting transfers between devices  46.7 us (6%)
  matrix products  40.1 us (5%)
  between operations  14.8 us (2%)
    psum x2, waiting for transfers between devices, process_desk(): carry_in = lax.psum(lax.psum(x_in, shard_axis), link_axis)  502 us
    scatter-add x15, other arithmetic, one_turn(): user_total = user_total.at[row_pick].add(forward * inverse)  49.1 us
    gather x15, local copies, waits for them, and re-layouts, one_turn(): user_source[row_pick]  27.1 us
    all_to_all x2, starting transfers between devices, summed_on_arrival(): lax.all_to_all(pieces, axis, split_axis=0, concat_axis=0, tiled=True)  24.1 us
    all_to_all x2, waiting for transfers between devices, summed_on_arrival(): lax.all_to_all(pieces, axis, split_axis=0, concat_axis=0, tiled=True)  22.7 us
    all_to_all x2, starting transfers between devices, from_everyone(): return lax.all_to_all(copies, axis, split_axis=0, concat_axis=0, tiled=True)  22.5 us
    select_n x30, other arithmetic, one_turn(): jnp.where(live_mask, 1.0 / norm_pick.astype(jnp.float32), 0.0)  21.7 us
    all_to_all x2, waiting for transfers between devices, from_everyone(): return lax.all_to_all(copies, axis, split_axis=0, concat_axis=0, tiled=True)  20.5 us
  transfers between devices with their start and end apart: 6, of which 4 were waited for; matrix products, arithmetic and copies ran while one was open for 23% of the time, Pallas kernels for 0%

profile of v1, /device:TPU:2, one launch (start us, length us, event | category | flops | bytes accessed | tf_op | source)
XLA Modules:
  0.0 793.0 jit_solution(13325222454458115610)
XLA Ops:
  7.2 2.0 broadcast_in_dim.43
  9.2 10.1 %all-to-all-start.2 = ((bf16[16,1,128,256]{3,2,1,0:T(8,128)(2,1)}), bf16[16,1,128,256]{3,2,1,0:T(8,128)(2,1)}, u32[]{:S(2)}, u32[]{:S(2)}) async-start(bf16[16,1,128,256]{3,2,1,0:T(8,128)(2,1)} %broadcast_in_dim.43), calls=%async_computation.2 | async-start | bytes 2097152 | tf_op jit(solution)/shard_map/all_to_all | solution.py:17
  20.0 6.4 copy.16
  26.3 20.5 %all-to-all-done.2 = bf16[16,1,128,256]{3,2,1,0:T(8,128)(2,1)} async-done(((bf16[16,1,128,256]{3,2,1,0:T(8,128)(2,1)}), bf16[16,1,128,256]{3,2,1,0:T(8,128)(2,1)}, u32[]{:S(2)}, u32[]{:S(2)}) %all-to-all-start.2) | async-done | bytes 1048608 | tf_op jit(solution)/shard_map/all_to_all | solution.py:17
  47.7 12.4 %all-to-all-start = ((bf16[32,1,32,256]{3,2,1,0:T(8,128)(2,1)}), bf16[32,1,32,256]{3,2,1,0:T(8,128)(2,1)S(1)}, u32[]{:S(2)}, u32[]{:S(2)}) async-start(bf16[32,1,32,256]{3,2,1,0:T(8,128)(2,1)} %broadcast_in_dim.40), calls=%async_computation | async-start | bytes 1048576 | tf_op jit(solution)/shard_map/all_to_all | solution.py:17
  60.3 78.4 %while.21 = (s32[]{:T(128)}, f32[8,128,256]{2,1,0:T(8,128)S(1)}, s32[]{:T(128)}, s32[128]{0:T(128)S(1)}, bf16[128,128,128]{1,2,0:T(8,128)(2,1)}, /*index=5*/s32[...) while((s32[]{:T(128)}, f32[8,128,256]{2,1,0:T(8,128)S(1)}, ...), condition=%wide.region_6.7_spmd, body=%wide.region_4.6_spmd.sunk | while | flops 67634272 | bytes 6033919 | solution.py:96
  61.1 1.8 gather_fusion.1
  71.6 1.8 gather_fusion.1
  76.8 1.8 gather_fusion.1
  82.0 1.8 gather_fusion.1
  139.5 10.5 %all-to-all-start.3 = ((bf16[32,32,256]{2,1,0:T(8,128)(2,1)}), bf16[32,32,256]{2,1,0:T(8,128)(2,1)S(1)}, u32[]{:S(2)}, u32[]{:S(2)}) async-start(bf16[32,32,256]{2,1,0:T(8,128)(2,1)} %bitcast.11), calls=%async_computation.3 | async-start | bytes 1048576 | tf_op jit(solution)/shard_map/all_to_all | solution.py:39
  151.6 88.7 %while.20 = (s32[]{:T(128)}, f32[16,128,256]{2,1,0:T(8,128)}, s32[]{:T(128)}, s32[128]{0:T(128)S(1)}, bf16[128,128,128]{2,1,0:T(8,128)(2,1)}, /*index=5*/s32[128...) while((s32[]{:T(128)}, f32[16,128,256]{2,1,0:T(8,128)}, ...), condition=%wide.region_2.3_spmd, body=%wide.region_0.2_spmd.sunk | while | flops 67634272 | bytes 6033919 | solution.py:96
  154.3 3.2 scatter_fusion
  160.2 3.2 scatter_fusion
  166.0 3.3 scatter_fusion
  172.0 3.3 scatter_fusion
  177.9 3.3 scatter_fusion
  183.8 3.3 scatter_fusion
  189.7 3.3 scatter_fusion
  195.6 3.3 scatter_fusion
  201.6 3.2 scatter_fusion
  207.5 3.3 scatter_fusion
  213.4 3.3 scatter_fusion
  219.3 3.4 scatter_fusion
  225.3 3.2 scatter_fusion
  231.1 3.4 scatter_fusion
  237.1 3.2 scatter_fusion
  240.4 2.7 convert_element_type.37
  243.1 13.6 %all-to-all-start.1 = ((bf16[16,128,256]{2,1,0:T(8,128)(2,1)}), bf16[16,128,256]{2,1,0:T(8,128)(2,1)S(1)}, u32[]{:S(2)}, u32[]{:S(2)}) async-start(bf16[16,128,256]{2,1,0:T(8,128)(2,1)} %convert_element_type.37), calls=%async_computation.1 | async-start | bytes 2097152 | tf_op jit(solution)/shard_map/all_to_all | solution.py:39
  257.1 22.7 %all-to-all-done.1 = bf16[16,128,256]{2,1,0:T(8,128)(2,1)S(1)} async-done(((bf16[16,128,256]{2,1,0:T(8,128)(2,1)}), bf16[16,128,256]{2,1,0:T(8,128)(2,1)S(1)}, u32[]{:S(2)}, u32[]{:S(2)}) %all-to-all-start.1) | async-done | bytes 1048608 | tf_op jit(solution)/shard_map/all_to_all | solution.py:39
  281.0 179.6 %all-reduce.3.cloned.1.call-done = f32[256,256]{0,1:T(8,128)} async-done(((f32[256,256]{0,1:T(8,128)}), f32[256,256]{0,1:T(8,128)}) %all-reduce.3.cloned.1.call-update) | async-done | bytes 262160 | tf_op jit(solution)/shard_map/psum | solution.py:11
  462.3 322.0 %all-reduce.5.cloned.1.call-done = f32[256,256]{0,1:T(8,128)} async-done(((f32[256,256]{0,1:T(8,128)}), f32[256,256]{0,1:T(8,128)}) %all-reduce.5.cloned.1.call-update) | async-done | bytes 262160 | tf_op jit(solution)/shard_map/psum | solution.py:11
  (193 shorter events, 118.3 us)
Async XLA Ops:
  7.2 453.5 %copy-start = (bf16[256,256]{1,0:T(8,128)(2,1)S(1)}, bf16[256,256]{1,0:T(8,128)(2,1)}, u32[]{:S(2)}) copy-start(bf16[256,256]{1,0:T(8,128)(2,1)} %param.16) | copy-start | bytes 393220
  9.2 37.7 %all-to-all-start.2 = ((bf16[16,1,128,256]{3,2,1,0:T(8,128)(2,1)}), bf16[16,1,128,256]{3,2,1,0:T(8,128)(2,1)}, u32[]{:S(2)}, u32[]{:S(2)}) async-start(bf16[16,1,128,256]{3,2,1,0:T(8,128)(2,1)} %broadcast_in_dim.43), calls=%async_computation.2 | async-start | bytes 2097152 | tf_op jit(solution)/shard_map/all_to_all | solution.py:17
  19.9 26.9 %copy-start.5 = (bf16[1,32,256]{2,1,0:T(8,128)(2,1)S(1)}, bf16[1,32,256]{2,1,0:T(8,128)(2,1)}, u32[]{:S(2)}) copy-start(bf16[1,32,256]{2,1,0:T(8,128)(2,1)} %param.18) | copy-start | bytes 49156
  26.3 33.9 %copy-start.2 = (s32[1,128]{1,0:T(1,128)S(1)}, s32[1,128]{1,0:T(1,128)}, u32[]{:S(2)}) copy-start(s32[1,128]{1,0:T(1,128)} %param.20) | copy-start | bytes 1540
  26.3 33.9 %copy-start.3 = (s32[1,128]{1,0:T(1,128)S(1)}, s32[1,128]{1,0:T(1,128)}, u32[]{:S(2)}) copy-start(s32[1,128]{1,0:T(1,128)} %param.21) | copy-start | bytes 1540
  26.3 34.0 %copy-start.4 = (s32[1,128]{1,0:T(1,128)S(1)}, s32[1,128]{1,0:T(1,128)}, u32[]{:S(2)}) copy-start(s32[1,128]{1,0:T(1,128)} %param.22) | copy-start | bytes 1540
  47.7 91.8 %all-to-all-start = ((bf16[32,1,32,256]{3,2,1,0:T(8,128)(2,1)}), bf16[32,1,32,256]{3,2,1,0:T(8,128)(2,1)S(1)}, u32[]{:S(2)}, u32[]{:S(2)}) async-start(bf16[32,1,32,256]{3,2,1,0:T(8,128)(2,1)} %broadcast_in_dim.40), calls=%async_computation | async-start | bytes 1048576 | tf_op jit(solution)/shard_map/all_to_all | solution.py:17
  139.5 103.5 %all-to-all-start.3 = ((bf16[32,32,256]{2,1,0:T(8,128)(2,1)}), bf16[32,32,256]{2,1,0:T(8,128)(2,1)S(1)}, u32[]{:S(2)}, u32[]{:S(2)}) async-start(bf16[32,32,256]{2,1,0:T(8,128)(2,1)} %bitcast.11), calls=%async_computation.3 | async-start | bytes 1048576 | tf_op jit(solution)/shard_map/all_to_all | solution.py:39
  243.1 13.7 %copy-start.6 = (bf16[1,32,256]{2,1,0:T(8,128)(2,1)S(1)}, bf16[1,32,256]{2,1,0:T(8,128)(2,1)}, u32[]{:S(2)}) copy-start(bf16[1,32,256]{2,1,0:T(8,128)(2,1)} %param.15) | copy-start | bytes 49156
  243.1 36.8 %copy-start.1 = (bf16[1,128,256]{2,1,0:T(8,128)(2,1)S(1)}, bf16[1,128,256]{2,1,0:T(8,128)(2,1)}, u32[]{:S(2)}) copy-start(bf16[1,128,256]{2,1,0:T(8,128)(2,1)} %param.14) | copy-start | bytes 196612
  243.1 36.7 %all-to-all-start.1 = ((bf16[16,128,256]{2,1,0:T(8,128)(2,1)}), bf16[16,128,256]{2,1,0:T(8,128)(2,1)S(1)}, u32[]{:S(2)}, u32[]{:S(2)}) async-start(bf16[16,128,256]{2,1,0:T(8,128)(2,1)} %convert_element_type.37), calls=%async_computation.1 | async-start | bytes 2097152 | tf_op jit(solution)/shard_map/all_to_all | solution.py:39
  256.6 204.0 %all-reduce.3.cloned.1.call-start = ((), (), s32[]{:S(2)}) async-start(), calls=%async_computation.4 | async-start | bytes 524288 | tf_op jit(solution)/shard_map/psum | solution.py:11
  280.9 503.4 %all-reduce.5.cloned.1.call-start = ((), (), s32[]{:S(2)}) async-start(), calls=%async_computation.5 | async-start | bytes 524288 | tf_op jit(solution)/shard_map/psum | solution.py:11
Sparse Core Ops, SparseCore 0:
  281.1 179.5 all-reduce.2
  463.5 320.7 all-reduce.4
